TPU v7x, 32 devices: a whole 2x2x4 slice. The times are simulated.
32 devices in a mesh: lon: 8 (over z, core), lat: 4 (over y, x).
Axes of the slice: x: 2, y: 2, z: 4, core: 2. Of those that a mesh axis runs over, the one named last changes fastest.
Arguments:
- head: float32 [4, 256, 16384], P(None, 'lat', 'lon'), may hold values from -6 to 6
- storage: float32 [4, 256, 16384], P(None, 'lat', 'lon'), may hold values from 0.5 to 2
- east_cond: float32 [4, 256, 16384], P(None, 'lat', 'lon'), may hold values from 0.1 to 1
- north_cond: float32 [4, 256, 16384], P(None, 'lat', 'lon'), may hold values from 0.1 to 1
- leakance: float32 [3, 256, 16384], P(None, 'lat', 'lon'), may hold values from 0.1 to 1
- recharge: float32 [4, 256, 16384], P(None, 'lat', 'lon'), may hold values from -12 to 12
- recoverable_skeleton_coefs: float32 [3, 256, 16384], P(None, 'lat', 'lon'), may hold values from 0.5 to 2
- permanent_skeleton_coefs: float32 [3, 256, 16384], P(None, 'lat', 'lon'), may hold values from 1 to 4
- critical_heads: float32 [3, 256, 16384], P(None, 'lat', 'lon'), may hold values from -4 to 4
- kernel: float32 [3, 1024], replicated, may hold values from -0.109375 to 0.109375
- land_tiles: int32 [4, 256], P('lat', 'lon'), may hold values 0 or 1
- cell_flags: int32 [4, 256, 16384], P(None, 'lat', 'lon'), may hold values 0 or 1
Outputs:
- new_head: float32 [4, 256, 16384], P(None, 'lat', 'lon')
- new_precon: float32 [3, 256, 16384], P(None, 'lat', 'lon')
- displacement: float32 [256, 16384], P('lat', 'lon')
All inputs are finite; a program needn't handle non-finite values. No bound on the sum of `land_tiles` or of `cell_flags` on one device may be relied on, other than what follows from the above.
Results may differ from a plain program's by a relative error of at most 0.0003.
Values sent between devices are 32-bit elements; how exact they have to be, the bound alone decides.
A program may use at most 192 MiB of HBM per device.

v0:
```python
import jax
import jax.numpy as jnp
from jax import lax
from jax.sharding import PartitionSpec as P

ITERS = 2


def from_behind(value, axis, steps):
    count = lax.axis_size(axis)
    pairs = [(source, (source + steps) % count) for source in range(count)]
    return lax.ppermute(value, axis, pairs)


def shifted(block, axis, distance):
    devices = range(lax.axis_size(axis))
    route = [(i - distance, i) for i in devices if i - distance in devices]
    return lax.ppermute(block, axis, route)


def with_halo(value, sides, width, wrap):
    for axis, dim in sides:
        size, length = (lax.axis_size(axis), value.shape[dim])
        up = [(i, (i + 1) % size) for i in range(size if wrap else size - 1)]
        down = [(j, i) for i, j in up]
        last = lax.slice_in_dim(value, length - width, length, axis=dim)
        initial = lax.slice_in_dim(value, 0, width, axis=dim)
        before = lax.ppermute(last, axis, up)
        after = lax.ppermute(initial, axis, down)
        value = jnp.concatenate([before, value, after], axis=dim)
    return value


def expand_tiles(land_tiles, tile):
    rows, cols = land_tiles.shape
    spread = jnp.broadcast_to(land_tiles[:, None, :, None], (rows, tile, cols, tile))
    return spread.reshape(rows * tile, cols * tile).astype(jnp.float32)


def toeplitz_table(kernel, tile):
    width = kernel.shape[1]
    place = (
        jnp.arange(width + tile, dtype=jnp.int32)[:, None]
        - jnp.arange(tile, dtype=jnp.int32)[None, :]
    )
    inside = (place >= 0) & (place < width)
    values = kernel[:, jnp.clip(place, 0, width - 1)]
    return jnp.where(inside[None], values, 0.0)


def convolve(enlarged_grid_map, table, columns, tile):
    count = columns // tile
    window = table.shape[1]

    def one_block(block):
        piece = lax.dynamic_slice_in_dim(enlarged_grid_map, block * tile, window, 2)
        return jnp.einsum("brp,bpc->rc", piece, table, precision=lax.Precision.HIGHEST)

    blocks = lax.map(one_block, jnp.arange(count, dtype=jnp.int32))
    return jnp.transpose(blocks, (1, 0, 2)).reshape(enlarged_grid_map.shape[1], columns)


def per_device(
    head,
    storage,
    east_cond,
    north_cond,
    leakance,
    recharge,
    recoverable_skeleton_coefs,
    permanent_skeleton_coefs,
    critical_heads,
    kernel,
    land_tiles,
    cell_flags,
):
    layers, rows, cols = head.shape
    tile = rows // land_tiles.shape[0]
    active = expand_tiles(land_tiles, tile)[None] * cell_flags.astype(jnp.float32)
    west_edge = from_behind(east_cond[:, :, -1:], "lon", 1)
    west_cond = jnp.concatenate([west_edge, east_cond[:, :, :-1]], axis=2)
    south_edge = shifted(north_cond[:, -1:, :], "lat", 1)
    south_cond = jnp.concatenate([south_edge, north_cond[:, :-1]], axis=1)
    zero_plane = jnp.zeros((1, rows, cols), jnp.float32)
    leak_up = jnp.concatenate([leakance, zero_plane], axis=0)
    leak_down = jnp.concatenate([zero_plane, leakance], axis=0)
    diagonal = storage + east_cond + west_cond + north_cond + south_cond + leak_up + leak_down

    def apply_op(field):
        masked = active * field
        lon_ext = with_halo(masked, (("lon", 2),), 1, True)
        lat_ext = with_halo(masked, (("lat", 1),), 1, False)
        upper_val = jnp.concatenate([masked[1:], zero_plane], axis=0)
        lower_val = jnp.concatenate([zero_plane, masked[:-1]], axis=0)
        beside = east_cond * lon_ext[:, :, 2:] + west_cond * lon_ext[:, :, :-2]
        beside = beside + north_cond * lat_ext[:, 2:] + south_cond * lat_ext[:, :-2]
        beside = beside + leak_up * upper_val + leak_down * lower_val
        return active * (diagonal * masked - beside) + (1.0 - active) * field

    def squares(residual):
        return lax.psum(jnp.sum(residual * residual), ("lon", "lat"))

    right = active * (storage * head + recharge) + (1.0 - active) * head
    solution = head
    residual = right - apply_op(head)
    direction = residual
    norm_now = squares(residual)
    for step in range(ITERS):
        image = apply_op(direction)
        alpha = norm_now / lax.psum(jnp.sum(direction * image), ("lon", "lat"))
        solution = solution + alpha * direction
        residual = residual - alpha * image
        norm_next = squares(residual)
        direction = residual + norm_next / norm_now * direction
        norm_now = norm_next
    paired_portions = active[:-1] * active[1:]
    prior_centre_heads = 0.5 * (head[:-1] + head[1:])
    renewed_centre_heads = 0.5 * (solution[:-1] + solution[1:])
    clay_lens_subsidence = paired_portions * (
        recoverable_skeleton_coefs * (prior_centre_heads - renewed_centre_heads)
        + permanent_skeleton_coefs
        * (
            jax.nn.relu(critical_heads - renewed_centre_heads)
            - jax.nn.relu(critical_heads - prior_centre_heads)
        )
    )
    new_precon = critical_heads - paired_portions * jax.nn.relu(
        critical_heads - renewed_centre_heads
    )
    width = kernel.shape[1]
    stencil_radius = width // 2
    table = toeplitz_table(kernel, tile)
    enlarged_grid_map = with_halo(clay_lens_subsidence, (("lon", 2),), stencil_radius, True)
    displacement = convolve(enlarged_grid_map, table, cols, tile)
    return (solution, new_precon, displacement)


def solution(mesh):
    placed = (
        P(None, "lat", "lon"),
        P(None, "lat", "lon"),
        P(None, "lat", "lon"),
        P(None, "lat", "lon"),
        P(None, "lat", "lon"),
        P(None, "lat", "lon"),
        P(None, "lat", "lon"),
        P(None, "lat", "lon"),
        P(None, "lat", "lon"),
        P(),
        P("lat", "lon"),
        P(None, "lat", "lon"),
    )
    return jax.shard_map(
        per_device,
        mesh=mesh,
        in_specs=placed,
        out_specs=(P(None, "lat", "lon"), P(None, "lat", "lon"), P("lat", "lon")),
        check_vma=False,
    )
```

profile of v0, /device:TPU:1, one launch (start us, length us, event | category | flops | bytes accessed | tf_op | source)
XLA Modules:
  0.0 572.7 jit_solution(2630525705447202528)
XLA Ops:
  1.4 2.7 fusion.50
  5.1 2.7 collective-permute-start.3
  9.1 4.6 collective-permute-start.5
  13.7 1.6 slice.138
  16.7 3.9 fusion.59
  21.6 3.4 collective-permute-start.1
  25.3 229.4 %gather_fusion = f32[69632,3]{1,0:T(8,128)} fusion(f32[3,1024]{0,1:T(8,128)S(1)} %copy.18, s32[69632]{0:T(1024)S(1)} %broadcast_clamp_fusion), kind=kCustom, calls=%fused_computation | custom fusion | bytes 1949696 | tf_op jit(solution)/shard_map/gather | solution.py:47
  254.8 14.1 %fusion.48 = (f32[4,64,2048]{2,1,0:T(8,128)S(1)}, f32[4,64,2048]{2,1,0:T(8,128)S(1)}) fusion(f32[4,64,2048]{2,1,0:T(8,128)S(1)} %get-tuple-element.49, f32[3,64,2048]{2,1,0:T(8,128)} %get-tuple-element.69, f32[3,64,2048]{2,1,0:T(8,128)} %get-tuple-element.68, f32[4,64,2048]{2,1,0:T(8,128)} %copy-done.8, f32[4,1,2048]{2,1,0:T(1,128)} %collective-permute-done.5, ...), kind=kLoop, calls=%fused_computation.89 | loop fusion | flops 18350080 | bytes 27854848 | tf_op jit(solution)/shard_map/mul | solution.py:90
  269.1 1.7 collective-permute-start.6
  272.2 4.3 collective-permute-start.9
  277.9 6.8 %multiply_reduce_fusion.1 = (f32[]{:T(128)}, f32[]{:T(128)}, f32[4,64,2048]{2,1,0:T(8,128)}) fusion(f32[4,64,2048]{2,1,0:T(8,128)S(1)} %get-tuple-element.47, f32[4,64,2048]{2,1,0:T(8,128)S(1)} %get-tuple-element.49, f32[3,64,2048]{2,1,0:T(8,128)} %get-tuple-element.63, f32[3,64,2048]{2,1,0:T(8,128)S(1)} %get-tuple-element.62, ...), kind=kLoop, calls=%fused_computation.71 | loop fusion | flops 17301502 | bytes 23660552 | tf_op jit(solution)/shard_map/reduce_sum | solution.py:110
  284.7 42.4 %all-reduce.8 = (f32[]{:T(128)}, f32[]{:T(128)}) all-reduce(f32[]{:T(128)} %get-tuple-element.32, f32[]{:T(128)} %get-tuple-element.31), channel_id=1, replica_groups=mesh['lon'=8,'lat'=4] {'lon','lat'}, use_global_device_ids=true, to_apply=%region_1.0 | all-reduce | flops 2 | bytes 16 | tf_op jit(solution)/shard_map/psum | solution.py:101
  328.5 3.4 multiply_reduce_fusion
  331.9 21.2 %copy.19 = f32[1088,64,3]{0,1,2:T(8,128)S(1)} copy(f32[1088,64,3]{2,1,0:T(8,128)} %bitcast.29) | data formatting | bytes 1671168 | tf_op jit(solution)/shard_map/gather | solution.py:47
  353.1 42.3 %psum.30 = f32[]{:T(128)} all-reduce(f32[]{:T(128)} %multiply_reduce_fusion), channel_id=1, replica_groups=mesh['lon'=8,'lat'=4] {'lon','lat'}, use_global_device_ids=true, to_apply=%region_5.0 | all-reduce | flops 1 | bytes 8 | tf_op jit(solution)/shard_map/psum | solution.py:101
  396.7 3.0 fusion.46
  403.0 4.5 collective-permute-start.13
  409.0 6.1 %fusion.20 = f32[]{:T(128)} fusion(f32[4,64,2048]{2,1,0:T(8,128)S(1)} %get-tuple-element.49, f32[3,64,2048]{2,1,0:T(8,128)S(1)} %copy-done.12, f32[4,64,2048]{2,1,0:T(8,128)S(1)} %fusion.46, f32[4,1,2048]{2,1,0:T(1,128)S(1)} %collective-permute-done.13, f32[4,64,2048]{2,1,0:T(8,128)S(1)} %copy-done.3, f32[4,1,2048]{2,1,0:T(1,128)S(1)} %collective-permute-done.12, ...), kind=kLoop, calls=%fused_computation.31 | loop fusion | flops 18350080 | bytes 23660556 | tf_op jit(solution)/shard_map/reduce_sum | solution.py:110
  415.1 40.1 %psum.31 = f32[]{:T(128)} all-reduce(f32[]{:T(128)} %fusion.20), channel_id=1, replica_groups=mesh['lon'=8,'lat'=4] {'lon','lat'}, use_global_device_ids=true, to_apply=%region_7.0 | all-reduce | flops 1 | bytes 8 | tf_op jit(solution)/shard_map/psum | solution.py:110
  456.5 3.7 multiply_add_fusion
  461.4 2.4 add_multiply_fusion
  463.8 2.9 collective-permute-start.14
  466.8 6.7 %collective-permute-done.14 = f32[3,64,512]{2,1,0:T(8,128)S(1)} collective-permute-done((f32[3,64,512]{2,1,0:T(8,128)S(1)}, f32[3,64,512]{2,1,0:T(8,128)S(1)}, u32[]{:S(2)}, u32[]{:S(2)}) %collective-permute-start.14) | collective-permute-done | bytes 393248 | tf_op jit(solution)/shard_map/ppermute | solution.py:28
  473.5 4.3 collective-permute-done.15
  478.0 91.8 %while.10 = (s32[]{:T(128)}, f32[32,64,64]{2,1,0:T(8,128)}, s32[32]{0:T(128)S(1)}, f32[3,64,3072]{2,1,0:T(8,128)S(1)}, f32[3,1088,64]{1,2,0:T(8,128)S(1)}, /*index=5*/s32[]{:T(128)}, s32[1]{0:T(128)}, s32[]{:T(128)}, s32[]{:T(128)}) while((s32[]{:T(128)}, f32[32,64,64]{2,1,0:T(8,128)}, s32[32]{0:T(128)S(1)}, f32[3,64,3072]{2,1,0:T(8,128)S(1)}, ...), condition=%wide.region_9.10_spmd, body=%wide.region_8.9_spmd.sunk | while | flops 160432128 | bytes 1802907 | solution.py:59
  484.9 1.6 fusion.67
  490.7 1.6 fusion.67
  493.5 1.6 fusion.67
  496.4 1.6 fusion.67
  499.3 1.6 fusion.67
  507.9 1.6 fusion.67
  513.6 1.6 fusion.67
  516.5 1.6 fusion.67
  519.4 1.6 fusion.67
  522.2 1.6 fusion.67
  530.8 1.6 fusion.67
  536.5 1.6 fusion.67
  539.4 1.6 fusion.67
  542.3 1.6 fusion.67
  545.2 1.6 fusion.67
  548.0 1.6 fusion.67
  553.8 1.6 fusion.67
  556.6 1.6 fusion.67
  559.5 1.6 fusion.67
  562.4 1.6 fusion.67
  565.2 1.6 fusion.67
  568.1 1.6 fusion.67
  569.7 1.8 copy.20
  (124 shorter events, 50.6 us)
Async XLA Ops:
  4.2 3.6 copy-start.8
  5.1 16.5 %collective-permute-start.2 = (f32[4,64,1]{2,1,0:T(8,128)}, f32[4,64,1]{2,1,0:T(8,128)S(1)}, u32[]{:S(2)}, u32[]{:S(2)}) collective-permute-start(f32[4,64,1]{2,1,0:T(8,128)} %get-tuple-element.64), channel_id=1, source_target_pairs={{4,0},{8,4},{12,8},{16,12},{20,16},{24,20},{28,24},{0,28},{5,1},{9... | collective-permute-start | bytes 3080 | tf_op jit(solution)/shard_map/ppermute | solution.py:29
  5.1 249.7 %collective-permute-start.3 = (f32[4,64,1]{2,1,0:T(8,128)}, f32[4,64,1]{2,1,0:T(8,128)}, u32[]{:S(2)}, u32[]{:S(2)}) collective-permute-start(f32[4,64,1]{2,1,0:T(8,128)} %get-tuple-element.65), channel_id=1, source_target_pairs={{0,4},{4,8},{8,12},{12,16},{16,20},{20,24},{24,28},{28,0},{1,5},{5... | collective-permute-start | bytes 3080 | tf_op jit(solution)/shard_map/ppermute | solution.py:28
  7.8 247.0 %collective-permute-start.4 = (f32[4,1,2048]{2,1,0:T(1,128)S(1)}, f32[4,1,2048]{2,1,0:T(1,128)}, u32[]{:S(2)}, u32[]{:S(2)}) collective-permute-start(f32[4,1,2048]{2,1,0:T(1,128)S(1)} %get-tuple-element.66), channel_id=1, source_target_pairs={{1,0},{2,1},{3,2},{5,4},{6,5},{7,6},{9,8},{10,9},{11,10},{13,12},{... | collective-permute-start | bytes 98312 | tf_op jit(solution)/shard_map/ppermute | solution.py:29
  9.1 245.7 %collective-permute-start.5 = (f32[4,1,2048]{2,1,0:T(1,128)S(1)}, f32[4,1,2048]{2,1,0:T(1,128)}, u32[]{:S(2)}, u32[]{:S(2)}) collective-permute-start(f32[4,1,2048]{2,1,0:T(1,128)S(1)} %get-tuple-element.67), channel_id=1, source_target_pairs={{0,1},{1,2},{2,3},{4,5},{5,6},{6,7},{8,9},{9,10},{10,11},{12,13},{... | collective-permute-start | bytes 98312 | tf_op jit(solution)/shard_map/ppermute | solution.py:28
  15.4 239.4 %collective-permute-start = (f32[4,64,1]{2,1,0:T(8,128)}, f32[4,64,1]{2,1,0:T(8,128)S(1)}, u32[]{:S(2)}, u32[]{:S(2)}) collective-permute-start(f32[4,64,1]{2,1,0:T(8,128)} %slice.138), channel_id=1, source_target_pairs={{0,4},{4,8},{8,12},{12,16},{16,20},{20,24},{24,28},{28,0},{1,5},{5... | collective-permute-start | bytes 3080 | tf_op jit(solution)/shard_map/ppermute | solution.py:12
  16.7 8.4 %copy-start.17 = (f32[3,1024]{1,0:T(4,128)S(1)}, f32[3,1024]{1,0:T(4,128)}, u32[]{:S(2)}) copy-start(f32[3,1024]{1,0:T(4,128)} %param.23) | copy-start | bytes 36868
  21.6 233.2 %collective-permute-start.1 = (f32[4,1,2048]{2,1,0:T(1,128)S(1)}, f32[4,1,2048]{2,1,0:T(1,128)S(1)}, u32[]{:S(2)}, u32[]{:S(2)}) collective-permute-start(f32[4,1,2048]{2,1,0:T(1,128)S(1)} %slice.140), channel_id=1, source_target_pairs={{0,1},{1,2},{2,3},{4,5},{5,6},{6,7},{8,9},{9,10},{10,11},{12,13},{... | collective-permute-start | bytes 98312 | tf_op jit(solution)/shard_map/ppermute | solution.py:18
  254.8 23.0 %copy-start.11 = (f32[3,64,2048]{2,1,0:T(8,128)S(1)}, f32[3,64,2048]{2,1,0:T(8,128)}, u32[]{:S(2)}) copy-start(f32[3,64,2048]{2,1,0:T(8,128)} %param.18) | copy-start | bytes 4718596
  268.9 8.9 %copy-start.4 = (f32[4,64,2048]{2,1,0:T(8,128)}, f32[4,64,2048]{2,1,0:T(8,128)S(1)}, u32[]{:S(2)}) copy-start(f32[4,64,2048]{2,1,0:T(8,128)S(1)} %get-tuple-element.47) | copy-start | bytes 6291460
  269.1 8.7 %collective-permute-start.6 = (f32[4,64,1]{2,1,0:T(8,128)S(1)}, f32[4,64,1]{2,1,0:T(8,128)S(1)}, u32[]{:S(2)}, u32[]{:S(2)}) collective-permute-start(f32[4,64,1]{2,1,0:T(8,128)S(1)} %get-tuple-element.58), channel_id=1, source_target_pairs={{4,0},{8,4},{12,8},{16,12},{20,16},{24,20},{28,24},{0,28},{5,1},{9... | collective-permute-start | bytes 3080 | tf_op jit(solution)/shard_map/ppermute | solution.py:29
  270.8 7.1 %collective-permute-start.7 = (f32[4,64,1]{2,1,0:T(8,128)S(1)}, f32[4,64,1]{2,1,0:T(8,128)S(1)}, u32[]{:S(2)}, u32[]{:S(2)}) collective-permute-start(f32[4,64,1]{2,1,0:T(8,128)S(1)} %get-tuple-element.59), channel_id=1, source_target_pairs={{0,4},{4,8},{8,12},{12,16},{16,20},{20,24},{24,28},{28,0},{1,5},{5... | collective-permute-start | bytes 3080 | tf_op jit(solution)/shard_map/ppermute | solution.py:28
  270.9 7.0 %collective-permute-start.8 = (f32[4,1,2048]{2,1,0:T(1,128)S(1)}, f32[4,1,2048]{2,1,0:T(1,128)S(1)}, u32[]{:S(2)}, u32[]{:S(2)}) collective-permute-start(f32[4,1,2048]{2,1,0:T(1,128)S(1)} %get-tuple-element.60), channel_id=1, source_target_pairs={{1,0},{2,1},{3,2},{5,4},{6,5},{7,6},{9,8},{10,9},{11,10},{13,12},{... | collective-permute-start | bytes 98312 | tf_op jit(solution)/shard_map/ppermute | solution.py:29
  272.2 5.7 copy-start
  272.2 5.7 copy-start.2
  272.2 5.7 copy-start.9
  272.2 5.6 collective-permute-start.9
  396.7 12.2 %copy-start.6 = (f32[4,64,2048]{2,1,0:T(8,128)S(1)}, f32[4,64,2048]{2,1,0:T(8,128)}, u32[]{:S(2)}) copy-start(f32[4,64,2048]{2,1,0:T(8,128)} %get-tuple-element.45) | copy-start | bytes 6291460
  396.7 12.2 %copy-start.10 = (f32[4,64,2048]{2,1,0:T(8,128)S(1)}, f32[4,64,2048]{2,1,0:T(8,128)}, u32[]{:S(2)}) copy-start(f32[4,64,2048]{2,1,0:T(8,128)} %param.15) | copy-start | bytes 6291460
  396.7 12.2 %copy-start.12 = (f32[3,64,2048]{2,1,0:T(8,128)S(1)}, f32[3,64,2048]{2,1,0:T(8,128)}, u32[]{:S(2)}) copy-start(f32[3,64,2048]{2,1,0:T(8,128)} %param.18) | copy-start | bytes 4718596
  399.9 9.0 %collective-permute-start.10 = (f32[4,64,1]{2,1,0:T(8,128)S(1)}, f32[4,64,1]{2,1,0:T(8,128)S(1)}, u32[]{:S(2)}, u32[]{:S(2)}) collective-permute-start(f32[4,64,1]{2,1,0:T(8,128)S(1)} %get-tuple-element.54), channel_id=1, source_target_pairs={{4,0},{8,4},{12,8},{16,12},{20,16},{24,20},{28,24},{0,28},{5,1},{9... | collective-permute-start | bytes 3080 | tf_op jit(solution)/shard_map/ppermute | solution.py:29
  401.2 7.7 %collective-permute-start.11 = (f32[4,64,1]{2,1,0:T(8,128)S(1)}, f32[4,64,1]{2,1,0:T(8,128)S(1)}, u32[]{:S(2)}, u32[]{:S(2)}) collective-permute-start(f32[4,64,1]{2,1,0:T(8,128)S(1)} %get-tuple-element.55), channel_id=1, source_target_pairs={{0,4},{4,8},{8,12},{12,16},{16,20},{20,24},{24,28},{28,0},{1,5},{5... | collective-permute-start | bytes 3080 | tf_op jit(solution)/shard_map/ppermute | solution.py:28
  401.7 7.2 %collective-permute-start.12 = (f32[4,1,2048]{2,1,0:T(1,128)S(1)}, f32[4,1,2048]{2,1,0:T(1,128)S(1)}, u32[]{:S(2)}, u32[]{:S(2)}) collective-permute-start(f32[4,1,2048]{2,1,0:T(1,128)S(1)} %get-tuple-element.56), channel_id=1, source_target_pairs={{1,0},{2,1},{3,2},{5,4},{6,5},{7,6},{9,8},{10,9},{11,10},{13,12},{... | collective-permute-start | bytes 98312 | tf_op jit(solution)/shard_map/ppermute | solution.py:29
  403.0 6.0 %copy-start.1 = (f32[4,64,2048]{2,1,0:T(8,128)S(1)}, f32[4,64,2048]{2,1,0:T(8,128)}, u32[]{:S(2)}) copy-start(f32[4,64,2048]{2,1,0:T(8,128)} %param.16) | copy-start | bytes 6291460
  403.0 6.0 %copy-start.3 = (f32[4,64,2048]{2,1,0:T(8,128)S(1)}, f32[4,64,2048]{2,1,0:T(8,128)}, u32[]{:S(2)}) copy-start(f32[4,64,2048]{2,1,0:T(8,128)} %param.17) | copy-start | bytes 6291460
  403.0 6.0 %copy-start.5 = (f32[4,64,2048]{2,1,0:T(8,128)S(1)}, f32[4,64,2048]{2,1,0:T(8,128)}, u32[]{:S(2)}) copy-start(f32[4,64,2048]{2,1,0:T(8,128)} %copy-done.4) | copy-start | bytes 6291460
  403.0 5.9 %collective-permute-start.13 = (f32[4,1,2048]{2,1,0:T(1,128)S(1)}, f32[4,1,2048]{2,1,0:T(1,128)S(1)}, u32[]{:S(2)}, u32[]{:S(2)}) collective-permute-start(f32[4,1,2048]{2,1,0:T(1,128)S(1)} %get-tuple-element.57), channel_id=1, source_target_pairs={{0,1},{1,2},{2,3},{4,5},{5,6},{6,7},{8,9},{9,10},{10,11},{12,13},{... | collective-permute-start | bytes 98312 | tf_op jit(solution)/shard_map/ppermute | solution.py:28
  456.5 3.8 copy-start.7
  456.5 3.9 copy-start.14
  456.5 4.4 copy-start.15
  456.5 4.8 copy-start.16
  461.3 2.4 copy-start.13
  463.8 9.7 %collective-permute-start.14 = (f32[3,64,512]{2,1,0:T(8,128)S(1)}, f32[3,64,512]{2,1,0:T(8,128)S(1)}, u32[]{:S(2)}, u32[]{:S(2)}) collective-permute-start(f32[3,64,512]{2,1,0:T(8,128)S(1)} %get-tuple-element.70), channel_id=1, source_target_pairs={{0,4},{4,8},{8,12},{12,16},{16,20},{20,24},{24,28},{28,0},{1,5},{5... | collective-permute-start | bytes 1179656 | tf_op jit(solution)/shard_map/ppermute | solution.py:28
  466.7 11.1 %collective-permute-start.15 = (f32[3,64,512]{2,1,0:T(8,128)S(1)}, f32[3,64,512]{2,1,0:T(8,128)S(1)}, u32[]{:S(2)}, u32[]{:S(2)}) collective-permute-start(f32[3,64,512]{2,1,0:T(8,128)S(1)} %get-tuple-element.71), channel_id=1, source_target_pairs={{4,0},{8,4},{12,8},{16,12},{20,16},{24,20},{28,24},{0,28},{5,1},{9... | collective-permute-start | bytes 1179656 | tf_op jit(solution)/shard_map/ppermute | solution.py:29
where the time goes:
time: 575 us; the launch traced here: 573 us
  local copies, waits for them, and re-layouts  285 us (50%)
  blocking collectives  125 us (22%)
  matrix products  52.1 us (9%)
  other arithmetic  43.2 us (8%)
  starting transfers between devices  30.9 us (5%)
  loops' own time  21 us (4%)
  waiting for transfers between devices  11 us (2%)
    gather x2, local copies, waits for them, and re-layouts, toeplitz_table(): values = kernel[:, jnp.clip(place, 0, width - 1)]  251 us
    psum x2, blocking collectives, squares(): return lax.psum(jnp.sum(residual * residual), ('lon', 'lat'))  84.7 us
    dot_general x32, matrix products, one_block(): jnp.einsum('brp,bpc->rc', piece, table, precision=lax.Precision.HIGHEST)  52.1 us
    psum x1, blocking collectives, per_device(): alpha = norm_now / lax.psum(jnp.sum(direction * image), ('lon', 'lat'))  40.1 us
    another operation x1, loops' own time, convolve(): blocks = lax.map(one_block, jnp.arange(count, dtype=jnp.int32))  21 us
    mul x3, other arithmetic, apply_op(): masked = active * field  19.8 us
    ppermute x7, starting transfers between devices, with_halo(): before = lax.ppermute(last, axis, up)  19.5 us
    dynamic_slice x32, local copies, waits for them, and re-layouts, convolve(): blocks = lax.map(one_block, jnp.arange(count, dtype=jnp.int32))  18.6 us
  transfers between devices with their start and end apart: 16, of which 2 were waited for; matrix products, arithmetic and copies ran while one was open for 42% of the time, Pallas kernels for 0%

commit v1 on v0

v1 whole, which is shorter than its diff:
```python
import functools

import jax
import jax.numpy as jnp
from jax import lax
from jax.experimental import pallas as pl
from jax.experimental.pallas import tpu as pltpu
from jax.sharding import PartitionSpec as P

MESH = pl.DeviceIdType.MESH
BLOCK = 256


def kernel(
    nlon, nlat,
    head, stor, east, north, leak, rech, rec, perm, crit, flags, ker, land,
    xo, po, do,
    HB, FL, S, E, N, K, Q, RC, PM, CR, M, U, R, W, FB, TH, TL, CH, CL, OUT, RX, DISP,
    scol, rcol, srow, rrow, snc, rnc, redA, redB,
    insem, outsem, hsend, hrecv, asend, arecv, bsend, brecv, dsend, drecv,
):
    L, rows, cols = HB.shape
    B = L - 1
    bands = rows // 8
    tile = cols // land.shape[1]
    width = ker.shape[1]
    lon, lat = lax.axis_index("lon"), lax.axis_index("lat")
    eastd = lax.rem(lon + 1, nlon)
    westd = lax.rem(lon + nlon - 1, nlon)
    northd = lax.rem(lat + 1, nlat)
    southd = lax.rem(lat + nlat - 1, nlat)
    mid = slice(128, 128 + cols)

    loads = [
        (head, HB), (flags, FL), (east, E.at[:, :, mid]), (north, N), (leak, K), (rech, Q),
        (stor, S), (rec, RC), (perm, PM), (crit, CR),
    ]
    loads = [pltpu.make_async_copy(a, b, insem.at[i]) for i, (a, b) in enumerate(loads)]
    for c in loads:
        c.start()

    barrier = pltpu.get_barrier_semaphore()
    for o in range(1, nlon):
        pl.semaphore_signal(barrier, inc=1, device_id={"lon": lax.rem(lon + o, nlon), "lat": lat}, device_id_type=MESH)
    for o in range(1, nlat):
        pl.semaphore_signal(barrier, inc=1, device_id={"lon": lon, "lat": lax.rem(lat + o, nlat)}, device_id_type=MESH)
    pl.semaphore_wait(barrier, nlon - 1 + nlat - 1)

    sub = lax.broadcasted_iota(jnp.int32, (8, cols), 0)
    lane = lax.broadcasted_iota(jnp.int32, (rows, 128), 1)
    lane1 = lax.broadcasted_iota(jnp.int32, (1, 128), 1)

    spread = (
        lax.broadcasted_iota(jnp.int32, (land.shape[1], cols), 1) // tile
        == lax.broadcasted_iota(jnp.int32, (land.shape[1], cols), 0)
    )
    land_row = jnp.dot(
        jnp.broadcast_to(land[...].astype(jnp.float32), (8, land.shape[1])),
        spread.astype(jnp.float32),
        preferred_element_type=jnp.float32,
    )

    def band(k):
        return pl.ds(pl.multiple_of(k * 8, 8), 8)

    loads[0].wait()
    loads[1].wait()

    @pl.loop(0, bands)
    def _(k):
        for l in range(L):
            m = land_row * FL[l, band(k), :].astype(jnp.float32)
            M[l, band(k), :] = m
            U[l, band(k), mid] = m * HB[l, band(k), :]

    def halo_copies(t):
        routes = [
            (scol.at[t, 0], rcol.at[t, 0], {"lon": eastd, "lat": lat}),
            (scol.at[t, 1], rcol.at[t, 1], {"lon": westd, "lat": lat}),
            (srow.at[t, 0], rrow.at[t, 0], {"lon": lon, "lat": northd}),
            (srow.at[t, 1], rrow.at[t, 1], {"lon": lon, "lat": southd}),
        ]
        if t == 0:
            routes.append((snc, rnc, {"lon": lon, "lat": northd}))
        return [
            pltpu.make_async_remote_copy(
                src_ref=s, dst_ref=d, send_sem=hsend.at[t, i], recv_sem=hrecv.at[t, i],
                device_id=to, device_id_type=MESH,
            )
            for i, (s, d, to) in enumerate(routes)
        ]

    def pack(t, ref):
        last = jnp.zeros((rows, 128), jnp.float32)
        first = jnp.zeros((rows, 128), jnp.float32)
        for l in range(L):
            tail = ref[l, 0:rows, cols:cols + 128]
            last = jnp.where(lane == l, pltpu.roll(tail, (l + 1) % 128, 1), last)
            start = ref[l, 0:rows, 128:256]
            first = jnp.where(lane == l, start if l == 0 else pltpu.roll(start, l, 1), first)
            srow[t, 0, l:l + 1, :] = ref[l, rows - 8:rows, mid][7:8, :]
            srow[t, 1, l:l + 1, :] = ref[l, 0:8, mid][0:1, :]
            if t == 0:
                tail = E[l, :, cols:cols + 128]
                last = jnp.where(lane == L + l, pltpu.roll(tail, (L + l + 1) % 128, 1), last)
                snc[l:l + 1, :] = N[l, rows - 8:rows, :][7:8, :]
        scol[t, 0] = last
        scol[t, 1] = first

    def send_halo(t, ref):
        pack(t, ref)
        copies = halo_copies(t)
        for c in copies:
            c.start()
        return copies

    has_south = (lat > 0).astype(jnp.float32)
    has_north = (lat < nlat - 1).astype(jnp.float32)

    def take_halo(t, ref, copies):
        for c in copies:
            c.wait()
        if t == 0:
            for l in range(L):
                E[l, :, 0:128] = jnp.broadcast_to(rcol[0, 0][:, L + l:L + l + 1], (rows, 128))
        for l in range(L):
            ref[l, 0:rows, 0:128] = jnp.broadcast_to(rcol[t, 0][:, l:l + 1], (rows, 128))
            ref[l, 0:rows, cols + 128:cols + 256] = jnp.broadcast_to(rcol[t, 1][:, l:l + 1], (rows, 128))
            ref[l, rows:rows + 8, mid] = jnp.broadcast_to(rrow[t, 1, l:l + 1, :] * has_north, (8, cols))
            below = (rnc[l:l + 1, :] * has_south) * (rrow[t, 0, l:l + 1, :] - ref[l, 0:8, mid][0:1, :])
            FB[l] = jnp.broadcast_to(below, (8, cols))

    def divergence(ref, k):
        centre, out = [], []
        for l in range(L):
            u = ref[l, band(k), :]
            e = E[l, band(k), :]
            ue = pltpu.roll(u, cols + 255, 1)
            fe = e * (u[:, :cols + 128] - ue[:, :cols + 128])
            acc = fe[:, 128:] - pltpu.roll(fe, 1, 1)[:, 128:]
            uc = u[:, mid]
            nxt = ref[l, band(k + 1), mid]
            un = jnp.where(sub == 7, pltpu.roll(nxt, 7, 0), pltpu.roll(uc, 7, 0))
            fn = N[l, band(k), :] * (uc - un)
            rf = pltpu.roll(fn, 1, 0)
            acc = acc + fn - jnp.where(sub == 0, FB[l], rf)
            FB[l] = rf
            if l > 0:
                fv = K[l - 1, band(k), :] * (centre[l - 1] - uc)
                out[l - 1] = out[l - 1] + fv
                acc = acc - fv
            centre.append(uc)
            out.append(acc)
        return centre, out

    def fold(v):
        total = v[:, 0:128]
        for c in range(128, cols, 128):
            total = total + v[:, c:c + 128]
        return total

    def all_reduce(t, va, vb):
        a = jnp.sum(va, axis=0, keepdims=True)
        b = jnp.sum(vb, axis=0, keepdims=True)
        v = jnp.where(lane1 < 64, a + pltpu.roll(a, 64, 1), b + pltpu.roll(b, 64, 1))
        redA[t, lon] = v

        def lon_copy(o):
            return pltpu.make_async_remote_copy(
                src_ref=redA.at[t, lon], dst_ref=redA.at[t, lon], send_sem=asend.at[t, o], recv_sem=arecv.at[t, o],
                device_id={"lon": lax.rem(lon + o, nlon), "lat": lat}, device_id_type=MESH,
            )

        def lat_copy(o):
            return pltpu.make_async_remote_copy(
                src_ref=redB.at[t, lat], dst_ref=redB.at[t, lat], send_sem=bsend.at[t, o], recv_sem=brecv.at[t, o],
                device_id={"lon": lon, "lat": lax.rem(lat + o, nlat)}, device_id_type=MESH,
            )

        first = [lon_copy(o) for o in range(1, nlon)]
        second = [lat_copy(o) for o in range(1, nlat)]

        def start():
            for c in first:
                c.start()

        def middle():
            for c in first:
                c.wait()
            redB[t, lat] = jnp.sum(redA[t], axis=0)
            for c in second:
                c.start()

        def finish():
            for c in second:
                c.wait()
            total = jnp.sum(redB[t], axis=0)
            a = jnp.sum(jnp.where(lane1 < 64, total, 0.0), axis=1, keepdims=True)
            b = jnp.sum(jnp.where(lane1 < 64, 0.0, total), axis=1, keepdims=True)
            return a, b

        return start, middle, finish

    zero = jnp.zeros((8, 128), jnp.float32)
    loads[2].wait()
    loads[3].wait()
    copies = send_halo(0, U)
    loads[4].wait()
    loads[5].wait()
    take_halo(0, U, copies)

    @pl.loop(0, bands)
    def _(k):
        _, out = divergence(U, k)
        for l in range(L):
            R[l, band(k), mid] = M[l, band(k), :] * (Q[l, band(k), :] - out[l])

    copies = send_halo(1, R)
    loads[6].wait()
    take_halo(1, R, copies)

    def second(k, carry):
        a, b = carry
        centre, out = divergence(R, k)
        for l in range(L):
            r = centre[l]
            w = M[l, band(k), :] * (S[l, band(k), :] * r + out[l])
            W[l, band(k), mid] = w
            a = a + fold(r * r)
            b = b + fold(r * w)
        return a, b

    a, b = lax.fori_loop(0, bands, second, (zero, zero))
    start, middle, finish = all_reduce(0, a, b)
    start()
    copies = send_halo(2, W)
    take_halo(2, W, copies)
    middle()

    @pl.loop(0, bands)
    def _(k):
        centre, out = divergence(W, k)
        for l in range(L):
            Q[l, band(k), :] = M[l, band(k), :] * (S[l, band(k), :] * centre[l] + out[l])

    rr0, bend = finish()
    alpha0 = rr0 / bend
    alpha_row = jnp.broadcast_to(alpha0, (8, 128))
    alpha_row = jnp.concatenate([alpha_row] * (cols // 128), axis=1)

    def third(k, carry):
        a, b = carry
        for l in range(L):
            w = W[l, band(k), mid]
            r1 = R[l, band(k), mid] - alpha_row * w
            s1 = w - alpha_row * Q[l, band(k), :]
            a = a + fold(r1 * r1)
            b = b + fold(r1 * s1)
        return a, b

    a, b = lax.fori_loop(0, bands, third, (zero, zero))
    start, middle, finish = all_reduce(1, a, b)
    start()

    half = width // 2
    h = half // BLOCK
    nb = cols // BLOCK
    lags = width // 128
    sides = BLOCK // 128

    def piece(b, e):
        if e < 0 or e >= lags:
            return jnp.zeros((1, 128), jnp.float32)
        return ker[b:b + 1, e * 128:(e + 1) * 128]

    for e in range(-1, lags + 2):
        places = [
            (d, ph, jh) for d in range(-h, h + 1) for ph in range(sides) for jh in range(sides)
            if sides * (d + h) + ph - jh == e
        ]
        for b in range(B):
            if 0 <= e <= lags:
                base = jnp.concatenate([piece(b, e), piece(b, e - 1)], axis=1)
                wide = pltpu.roll(jnp.broadcast_to(base, (128, 256)), 0, 1, stride=1, stride_axis=0)
                block = wide[:, :128].T
            else:
                block = jnp.zeros((128, 128), jnp.float32)
            hi = block.astype(jnp.bfloat16)
            lo = (block - hi.astype(jnp.float32)).astype(jnp.bfloat16)
            for d, ph, jh in places:
                at = (d + h, slice(b * BLOCK + ph * 128, b * BLOCK + ph * 128 + 128), slice(jh * 128, jh * 128 + 128))
                TH[at] = hi
                TL[at] = lo

    for i in (7, 8, 9):
        loads[i].wait()
    middle()
    rr1, curve = finish()
    beta = rr1 / rr0
    alpha1 = rr1 / (curve - beta * rr1 / alpha0)
    of_r = jnp.broadcast_to(alpha0 + alpha1 + alpha1 * beta, (16, BLOCK))
    of_w = jnp.broadcast_to(alpha1 * alpha0, (16, BLOCK))

    @pl.loop(0, rows // 16)
    def _(k):
        r = pl.ds(pl.multiple_of(k * 16, 16), 16)
        for p in range(nb):
            cs = slice(p * BLOCK, (p + 1) * BLOCK)
            ps = slice(128 + p * BLOCK, 128 + (p + 1) * BLOCK)
            old = [HB[l, r, cs] for l in range(L)]
            new = [old[l] + of_r * R[l, r, ps] - of_w * W[l, r, ps] for l in range(L)]
            for l in range(L):
                HB[l, r, cs] = new[l]
            for b in range(B):
                both = M[b, r, cs] * M[b + 1, r, cs]
                om = 0.5 * (old[b] + old[b + 1])
                nm = 0.5 * (new[b] + new[b + 1])
                cr = CR[b, r, cs]
                over = jnp.maximum(cr - nm, 0.0)
                comp = both * (RC[b, r, cs] * (om - nm) + PM[b, r, cs] * (over - jnp.maximum(cr - om, 0.0)))
                CR[b, r, cs] = cr - both * over
                hi = comp.astype(jnp.bfloat16)
                lo = (comp - hi.astype(jnp.float32)).astype(jnp.bfloat16)
                dst = pl.ds(pl.multiple_of(p * rows + k * 16, 16), 16)
                CH[dst, b * BLOCK:(b + 1) * BLOCK] = hi
                CL[dst, b * BLOCK:(b + 1) * BLOCK] = lo

    outs = [pltpu.make_async_copy(HB, xo, outsem.at[0]), pltpu.make_async_copy(CR, po, outsem.at[1])]
    for c in outs:
        c.start()

    def product(d, low, high):
        ch, cl = CH[low * rows:high * rows, :], CL[low * rows:high * rows, :]
        th, tl = TH[d + h], TL[d + h]
        dot = functools.partial(jnp.dot, preferred_element_type=jnp.float32)
        return dot(ch, th) + (dot(ch, tl) + dot(cl, th))

    for d in range(h, 0, -1):
        left = product(d, 0, d)
        right = product(-d, nb - d, nb)
        at = slice((h - d) * rows, h * rows)
        end = slice((h + nb) * rows, (h + nb + d) * rows)
        if d == h:
            OUT[at, :] = left
            OUT[end, :] = right
        else:
            OUT[at, :] += left
            OUT[end, :] += right
    exts = [
        pltpu.make_async_remote_copy(
            src_ref=OUT.at[0:h * rows, :], dst_ref=RX.at[1], send_sem=dsend.at[0], recv_sem=drecv.at[0],
            device_id={"lon": westd, "lat": lat}, device_id_type=MESH,
        ),
        pltpu.make_async_remote_copy(
            src_ref=OUT.at[(h + nb) * rows:(2 * h + nb) * rows, :], dst_ref=RX.at[0], send_sem=dsend.at[1], recv_sem=drecv.at[1],
            device_id={"lon": eastd, "lat": lat}, device_id_type=MESH,
        ),
    ]
    for c in exts:
        c.start()
    OUT[h * rows:(h + nb) * rows, :] = product(0, 0, nb)
    for d in range(1, h + 1):
        OUT[h * rows:(h + nb - d) * rows, :] += product(d, d, nb)
        OUT[(h + d) * rows:(h + nb) * rows, :] += product(-d, 0, nb - d)
    for c in exts:
        c.wait()
    for p in range(nb):
        v = OUT[(h + p) * rows:(h + p + 1) * rows, :]
        if p < h:
            v = v + RX[0, p * rows:(p + 1) * rows, :]
        if p >= nb - h:
            q = p - (nb - h)
            v = v + RX[1, q * rows:(q + 1) * rows, :]
        DISP[:, p * BLOCK:(p + 1) * BLOCK] = v
    outs.append(pltpu.make_async_copy(DISP, do, outsem.at[2]))
    outs[2].start()
    for c in outs:
        c.wait()


def per_device(
    nlon, nlat, head, storage, east_cond, north_cond, leakance, recharge,
    recoverable_skeleton_coefs, permanent_skeleton_coefs, critical_heads, kernel_, land_tiles, cell_flags,
):
    L, rows, cols = head.shape
    B = L - 1
    width = kernel_.shape[1]
    f32 = jnp.float32
    full, inter = (L, rows, cols), (B, rows, cols)
    padded = (L, rows + 8, cols + 256)
    h = width // 2 // BLOCK
    nb = cols // BLOCK
    V = pltpu.VMEM
    dma = pltpu.SemaphoreType.DMA
    scratch = [
        V(full, f32), V(full, jnp.int32), V(full, f32), V((L, rows, cols + 128), f32), V(full, f32), V(inter, f32),
        V(full, f32), V(inter, f32), V(inter, f32), V(inter, f32), V(full, f32),
        V(padded, f32), V(padded, f32), V(padded, f32), V((L, 8, cols), f32),
        V((2 * h + 1, B * BLOCK, BLOCK), jnp.bfloat16), V((2 * h + 1, B * BLOCK, BLOCK), jnp.bfloat16),
        V((nb * rows, B * BLOCK), jnp.bfloat16), V((nb * rows, B * BLOCK), jnp.bfloat16),
        V(((nb + 2 * h) * rows, BLOCK), f32), V((2, h * rows, BLOCK), f32), V((rows, cols), f32),
        V((3, 2, rows, 128), f32), V((3, 2, rows, 128), f32),
        V((3, 2, L, cols), f32), V((3, 2, L, cols), f32), V((L, cols), f32), V((L, cols), f32),
        V((2, nlon, 1, 128), f32), V((2, nlat, 1, 128), f32),
        dma((10,)), dma((3,)), dma((3, 5)), dma((3, 5)), dma((2, nlon)), dma((2, nlon)), dma((2, nlat)), dma((2, nlat)),
        dma((2,)), dma((2,)),
    ]
    hbm = pl.BlockSpec(memory_space=pl.ANY)
    vmem = pl.BlockSpec(memory_space=pltpu.VMEM)
    return pl.pallas_call(
        functools.partial(kernel, nlon, nlat),
        out_shape=(
            jax.ShapeDtypeStruct(full, f32), jax.ShapeDtypeStruct(inter, f32), jax.ShapeDtypeStruct((rows, cols), f32),
        ),
        in_specs=[hbm] * 10 + [vmem] * 2,
        out_specs=(hbm,) * 3,
        scratch_shapes=scratch,
        name="aquifer_step",
        compiler_params=pltpu.CompilerParams(collective_id=0, has_side_effects=True, vmem_limit_bytes=60 * 1024 * 1024),
    )(
        head, storage, east_cond, north_cond, leakance, recharge, recoverable_skeleton_coefs,
        permanent_skeleton_coefs, critical_heads, cell_flags, kernel_, land_tiles,
    )


def solution(mesh):
    block = P(None, "lat", "lon")
    placed = (block,) * 9 + (P(), P("lat", "lon"), block)
    return jax.shard_map(
        functools.partial(per_device, mesh.shape["lon"], mesh.shape["lat"]),
        mesh=mesh,
        in_specs=placed,
        out_specs=(block, block, P("lat", "lon")),
        check_vma=False,
    )
```

time: 575 us -> 49.6 us (0.09)
  local copies, waits for them, and re-layouts: 285 us -> 5.45 us
  blocking collectives: 125 us -> 0 us
  matrix products: 52.1 us -> 0 us
  Pallas kernels: 0 us -> 43.3 us
  other arithmetic: 43.2 us -> 0 us
  starting transfers between devices: 30.9 us -> 0 us
  loops' own time: 21 us -> 0 us
  waiting for transfers between devices: 11 us -> 0 us
    gather x2 -> x0, local copies, waits for them, and re-layouts: 251 us -> none  [toeplitz_table(): values = kernel[:, jnp.clip(place, 0, width - 1)]]
    psum x3 -> x0, blocking collectives: 125 us -> none  [the longest x2 84.7 us: squares(): return lax.psum(jnp.sum(residual * residual), ('lon', 'lat'))]
    dot_general x32 -> x0, matrix products: 52.1 us -> none  [one_block(): jnp.einsum('brp,bpc->rc', piece, table, precision=lax.Precision.HIGHEST)]
    pallas_call x0 -> x1, Pallas kernels: none -> 43.3 us  [per_device(): pl.pallas_call(functools.partial(kernel, nlon, nlat), out_shape=(jax.Shap...]
    ppermute x16 -> x0, starting transfers between devices: 30.9 us -> none  [the longest x7 19.5 us: with_halo(): before = lax.ppermute(last, axis, up)]
    mul x4 -> x0, other arithmetic: 22.2 us -> none  [the longest x3 19.8 us: apply_op(): masked = active * field]
    another operation x1 -> x0, loops' own time: 21 us -> none  [convolve(): blocks = lax.map(one_block, jnp.arange(count, dtype=jnp.int32))]
    dynamic_slice x32 -> x0, local copies, waits for them, and re-layouts: 18.6 us -> none  [convolve(): blocks = lax.map(one_block, jnp.arange(count, dtype=jnp.int32))]
  transfers between devices with their start and end apart: 16 -> 0, of which waited for: 2 -> 0; matrix products, arithmetic and copies ran while one was open for 42% -> 0% of each run, Pallas kernels for 0% -> 0%
where the time goes in v1:
time: 49.6 us; the launch traced here: 49.4 us
  Pallas kernels  43.3 us (87%)
  local copies, waits for them, and re-layouts  5.45 us (11%)
  between operations  0.65 us (1%)
    pallas_call x1, Pallas kernels, per_device(): pl.pallas_call(functools.partial(kernel, nlon, nlat), out_shape=(jax.Shap...  43.3 us
    unnamed x7, local copies, waits for them, and re-layouts  5.45 us

profile of v1, /device:TPU:1, one launch (start us, length us, event | category | flops | bytes accessed | tf_op | source)
XLA Modules:
  0.0 49.4 jit_solution(8929050921605930601)
XLA Ops:
  0.6 43.3 %aquifer_step.1 = (f32[4,64,2048]{2,1,0:T(8,128)}, f32[3,64,2048]{2,1,0:T(8,128)}, f32[64,2048]{1,0:T(8,128)}) custom-call(f32[4,64,2048]{2,1,0:T(8,128)} %head.1, f32[4,64,2048]{2,1,0:T(8,128)} %stor.1, f32[4,64,2048]{2,1,0:T(8,128)} %east.1, f32[4,64,2048]{2,1,0:T(8,128)} %north.1, f32[3,64,2048]{2,1,0:T(8,128)} %leak.1, f32[4,64,2048]{2,1,0:T(8,128)} %rech.1, ...), custom_call_target="tpu_custom_call" | custom-call | tf_op jit(solution)/shard_map/aquifer_step/pallas_call | solution.py:410
  43.9 0.0 copy-start
  43.9 3.3 %copy.18 = f32[4,64,2048]{2,1,0:T(8,128)} copy(f32[4,64,2048]{2,1,0:T(8,128)} %get-tuple-element.6) | data formatting | bytes 4194304
  47.2 0.0 copy-done
  47.2 0.0 copy-start.1
  47.2 1.1 %copy.19 = f32[3,64,2048]{2,1,0:T(8,128)} copy(f32[3,64,2048]{2,1,0:T(8,128)S(1)} %copy-done) | data formatting | bytes 3145728
  48.3 0.3 copy-done.1
  48.6 0.8 %copy.20 = f32[64,2048]{1,0:T(8,128)} copy(f32[64,2048]{1,0:T(8,128)S(1)} %copy-done.1) | data formatting | bytes 1048576
Async XLA Ops:
  43.9 3.3 %copy-start = (f32[3,64,2048]{2,1,0:T(8,128)S(1)}, f32[3,64,2048]{2,1,0:T(8,128)}, u32[]{:S(2)}) copy-start(f32[3,64,2048]{2,1,0:T(8,128)} %get-tuple-element.7) | copy-start | bytes 4718596
  47.2 1.4 %copy-start.1 = (f32[64,2048]{1,0:T(8,128)S(1)}, f32[64,2048]{1,0:T(8,128)}, u32[]{:S(2)}) copy-start(f32[64,2048]{1,0:T(8,128)} %get-tuple-element.8) | copy-start | bytes 1572868

commit v2 on v1

--- a/solution.py
+++ b/solution.py
@@ -9,6 +9,7 @@
 
 MESH = pl.DeviceIdType.MESH
 BLOCK = 256
+GROUPS = 4
 
 
 def kernel(
@@ -31,20 +32,34 @@
     southd = lax.rem(lat + nlat - 1, nlat)
     mid = slice(128, 128 + cols)
 
-    loads = [
-        (head, HB), (flags, FL), (east, E.at[:, :, mid]), (north, N), (leak, K), (rech, Q),
-        (stor, S), (rec, RC), (perm, PM), (crit, CR),
+    def fetch(sem, a, b):
+        copy = pltpu.make_async_copy(a, b, insem.at[sem])
+        copy.start()
+        return copy
+
+    group = rows // GROUPS
+    early = [fetch(i, a, b) for i, (a, b) in enumerate(((head, HB), (flags, FL), (east, E.at[:, :, mid]), (north, N)))]
+    grouped = []
+    for g in range(GROUPS):
+        rs = slice(g * group, (g + 1) * group)
+        grouped.append([fetch(4 + 2 * g, leak.at[:, rs], K.at[:, rs]), fetch(5 + 2 * g, rech.at[:, rs], Q.at[:, rs])])
+    late = [
+        fetch(4 + 2 * GROUPS + i, a, b) for i, (a, b) in enumerate(((stor, S), (rec, RC), (perm, PM), (crit, CR)))
     ]
-    loads = [pltpu.make_async_copy(a, b, insem.at[i]) for i, (a, b) in enumerate(loads)]
-    for c in loads:
-        c.start()
 
     barrier = pltpu.get_barrier_semaphore()
     for o in range(1, nlon):
         pl.semaphore_signal(barrier, inc=1, device_id={"lon": lax.rem(lon + o, nlon), "lat": lat}, device_id_type=MESH)
     for o in range(1, nlat):
         pl.semaphore_signal(barrier, inc=1, device_id={"lon": lon, "lat": lax.rem(lat + o, nlat)}, device_id_type=MESH)
-    pl.semaphore_wait(barrier, nlon - 1 + nlat - 1)
+
+    for ref in (U, R, W):
+        for l in range(L):
+            ref[l, 0:rows, 0:128] = jnp.zeros((rows, 128), jnp.float32)
+            ref[l, 0:rows, cols + 128:cols + 256] = jnp.zeros((rows, 128), jnp.float32)
+            ref[l, rows:rows + 8, mid] = jnp.zeros((8, cols), jnp.float32)
+    for l in range(L):
+        E[l, :, 0:128] = jnp.zeros((rows, 128), jnp.float32)
 
     sub = lax.broadcasted_iota(jnp.int32, (8, cols), 0)
     lane = lax.broadcasted_iota(jnp.int32, (rows, 128), 1)
@@ -60,11 +75,13 @@
         preferred_element_type=jnp.float32,
     )
 
+    zero = jnp.zeros((8, 128), jnp.float32)
+
     def band(k):
         return pl.ds(pl.multiple_of(k * 8, 8), 8)
 
-    loads[0].wait()
-    loads[1].wait()
+    early[0].wait()
+    early[1].wait()
 
     @pl.loop(0, bands)
     def _(k):
@@ -109,26 +126,53 @@
 
     def send_halo(t, ref):
         pack(t, ref)
+        if t == 0:
+            pl.semaphore_wait(barrier, nlon - 1 + nlat - 1)
         copies = halo_copies(t)
         for c in copies:
             c.start()
+        for l in range(L):
+            if t == 0:
+                FB[l] = jnp.zeros((8, cols), jnp.float32)
+            else:
+                FB[l] = -jnp.broadcast_to((rnc[l:l + 1, :] * has_south) * ref[l, 0:8, mid][0:1, :], (8, cols))
         return copies
 
     has_south = (lat > 0).astype(jnp.float32)
     has_north = (lat < nlat - 1).astype(jnp.float32)
 
-    def take_halo(t, ref, copies):
+    def take_halo(t, ref, copies, dst, shift, sign):
         for c in copies:
             c.wait()
-        if t == 0:
-            for l in range(L):
+        dot = jnp.zeros((8, 128), jnp.float32)
+
+        def add(l, rs, c0, n, delta):
+            at = (l, rs, slice(c0 + shift, c0 + shift + n))
+            dst[at] = dst[at] + sign * (M[l, rs, c0:c0 + n] * delta)
+            part = ref[l, rs, 128 + c0:128 + c0 + n] * delta
+            total = zero
+            for r in range(0, part.shape[0], 8):
+                for c in range(0, n, 128):
+                    total = total + part[r:r + 8, c:c + 128]
+            return total
+
+        whole, last = slice(0, rows), cols - 128
+        for l in range(L):
+            far = jnp.broadcast_to(rcol[t, 0][:, l:l + 1], (rows, 128))
+            if t == 0:
                 E[l, :, 0:128] = jnp.broadcast_to(rcol[0, 0][:, L + l:L + l + 1], (rows, 128))
-        for l in range(L):
-            ref[l, 0:rows, 0:128] = jnp.broadcast_to(rcol[t, 0][:, l:l + 1], (rows, 128))
-            ref[l, 0:rows, cols + 128:cols + 256] = jnp.broadcast_to(rcol[t, 1][:, l:l + 1], (rows, 128))
-            ref[l, rows:rows + 8, mid] = jnp.broadcast_to(rrow[t, 1, l:l + 1, :] * has_north, (8, cols))
-            below = (rnc[l:l + 1, :] * has_south) * (rrow[t, 0, l:l + 1, :] - ref[l, 0:8, mid][0:1, :])
-            FB[l] = jnp.broadcast_to(below, (8, cols))
+                far = far - ref[l, 0:rows, 128:256]
+            dot = dot + add(l, whole, 0, 128, jnp.where(lane == 0, -E[l, :, 0:128] * far, 0.0))
+            far = jnp.broadcast_to(rcol[t, 1][:, l:l + 1], (rows, 128))
+            dot = dot + add(l, whole, last, 128, jnp.where(lane == 127, -E[l, :, cols:cols + 128] * far, 0.0))
+            far = jnp.broadcast_to(rrow[t, 0, l:l + 1, :] * has_south, (8, cols))
+            if t == 0:
+                far = far - ref[l, 0:8, mid]
+            cond = jnp.broadcast_to(rnc[l:l + 1, :] * has_south, (8, cols))
+            dot = dot + add(l, slice(0, 8), 0, cols, jnp.where(sub == 0, -cond * far, 0.0))
+            far = jnp.broadcast_to(rrow[t, 1, l:l + 1, :] * has_north, (8, cols))
+            dot = dot + add(l, slice(rows - 8, rows), 0, cols, jnp.where(sub == 7, -N[l, rows - 8:rows, :] * far, 0.0))
+        return dot
 
     def divergence(ref, k):
         centre, out = [], []
@@ -201,23 +245,22 @@
 
         return start, middle, finish
 
-    zero = jnp.zeros((8, 128), jnp.float32)
-    loads[2].wait()
-    loads[3].wait()
+    early[2].wait()
+    early[3].wait()
     copies = send_halo(0, U)
-    loads[4].wait()
-    loads[5].wait()
-    take_halo(0, U, copies)
-
-    @pl.loop(0, bands)
-    def _(k):
-        _, out = divergence(U, k)
-        for l in range(L):
-            R[l, band(k), mid] = M[l, band(k), :] * (Q[l, band(k), :] - out[l])
-
+    for g in range(GROUPS):
+        for c in grouped[g]:
+            c.wait()
+
+        @pl.loop(g * bands // GROUPS, (g + 1) * bands // GROUPS)
+        def _(k):
+            _, out = divergence(U, k)
+            for l in range(L):
+                R[l, band(k), mid] = M[l, band(k), :] * (Q[l, band(k), :] - out[l])
+
+    take_halo(0, U, copies, R, 128, -1.0)
     copies = send_halo(1, R)
-    loads[6].wait()
-    take_halo(1, R, copies)
+    late[0].wait()
 
     def second(k, carry):
         a, b = carry
@@ -231,11 +274,10 @@
         return a, b
 
     a, b = lax.fori_loop(0, bands, second, (zero, zero))
+    b = b + take_halo(1, R, copies, W, 128, 1.0)
     start, middle, finish = all_reduce(0, a, b)
     start()
     copies = send_halo(2, W)
-    take_halo(2, W, copies)
-    middle()
 
     @pl.loop(0, bands)
     def _(k):
@@ -243,6 +285,8 @@
         for l in range(L):
             Q[l, band(k), :] = M[l, band(k), :] * (S[l, band(k), :] * centre[l] + out[l])
 
+    middle()
+    take_halo(2, W, copies, Q, 0, 1.0)
     rr0, bend = finish()
     alpha0 = rr0 / bend
     alpha_row = jnp.broadcast_to(alpha0, (8, 128))
@@ -292,8 +336,8 @@
                 TH[at] = hi
                 TL[at] = lo
 
-    for i in (7, 8, 9):
-        loads[i].wait()
+    for c in late[1:]:
+        c.wait()
     middle()
     rr1, curve = finish()
     beta = rr1 / rr0
@@ -301,33 +345,33 @@
     of_r = jnp.broadcast_to(alpha0 + alpha1 + alpha1 * beta, (16, BLOCK))
     of_w = jnp.broadcast_to(alpha1 * alpha0, (16, BLOCK))
 
-    @pl.loop(0, rows // 16)
-    def _(k):
-        r = pl.ds(pl.multiple_of(k * 16, 16), 16)
-        for p in range(nb):
-            cs = slice(p * BLOCK, (p + 1) * BLOCK)
-            ps = slice(128 + p * BLOCK, 128 + (p + 1) * BLOCK)
-            old = [HB[l, r, cs] for l in range(L)]
-            new = [old[l] + of_r * R[l, r, ps] - of_w * W[l, r, ps] for l in range(L)]
-            for l in range(L):
-                HB[l, r, cs] = new[l]
-            for b in range(B):
-                both = M[b, r, cs] * M[b + 1, r, cs]
-                om = 0.5 * (old[b] + old[b + 1])
-                nm = 0.5 * (new[b] + new[b + 1])
-                cr = CR[b, r, cs]
-                over = jnp.maximum(cr - nm, 0.0)
-                comp = both * (RC[b, r, cs] * (om - nm) + PM[b, r, cs] * (over - jnp.maximum(cr - om, 0.0)))
-                CR[b, r, cs] = cr - both * over
-                hi = comp.astype(jnp.bfloat16)
-                lo = (comp - hi.astype(jnp.float32)).astype(jnp.bfloat16)
-                dst = pl.ds(pl.multiple_of(p * rows + k * 16, 16), 16)
-                CH[dst, b * BLOCK:(b + 1) * BLOCK] = hi
-                CL[dst, b * BLOCK:(b + 1) * BLOCK] = lo
-
-    outs = [pltpu.make_async_copy(HB, xo, outsem.at[0]), pltpu.make_async_copy(CR, po, outsem.at[1])]
-    for c in outs:
-        c.start()
+    def compact(blocks):
+        @pl.loop(0, rows // 16)
+        def _(k):
+            r = pl.ds(pl.multiple_of(k * 16, 16), 16)
+            for p in blocks:
+                cs = slice(p * BLOCK, (p + 1) * BLOCK)
+                ps = slice(128 + p * BLOCK, 128 + (p + 1) * BLOCK)
+                old = [HB[l, r, cs] for l in range(L)]
+                new = [old[l] + of_r * R[l, r, ps] - of_w * W[l, r, ps] for l in range(L)]
+                for l in range(L):
+                    xo[l, r, cs] = new[l]
+                for b in range(B):
+                    both = M[b, r, cs] * M[b + 1, r, cs]
+                    om = 0.5 * (old[b] + old[b + 1])
+                    nm = 0.5 * (new[b] + new[b + 1])
+                    cr = CR[b, r, cs]
+                    over = jnp.maximum(cr - nm, 0.0)
+                    comp = both * (RC[b, r, cs] * (om - nm) + PM[b, r, cs] * (over - jnp.maximum(cr - om, 0.0)))
+                    po[b, r, cs] = cr - both * over
+                    hi = comp.astype(jnp.bfloat16)
+                    lo = (comp - hi.astype(jnp.float32)).astype(jnp.bfloat16)
+                    dst = pl.ds(pl.multiple_of(p * rows + k * 16, 16), 16)
+                    CH[dst, b * BLOCK:(b + 1) * BLOCK] = hi
+                    CL[dst, b * BLOCK:(b + 1) * BLOCK] = lo
+
+    edge = [p for p in range(nb) if p < h or p >= nb - h]
+    compact(edge)
 
     def product(d, low, high):
         ch, cl = CH[low * rows:high * rows, :], CL[low * rows:high * rows, :]
@@ -358,6 +402,7 @@
     ]
     for c in exts:
         c.start()
+    compact([p for p in range(nb) if p not in edge])
     OUT[h * rows:(h + nb) * rows, :] = product(0, 0, nb)
     for d in range(1, h + 1):
         OUT[h * rows:(h + nb - d) * rows, :] += product(d, d, nb)
@@ -371,11 +416,7 @@
         if p >= nb - h:
             q = p - (nb - h)
             v = v + RX[1, q * rows:(q + 1) * rows, :]
-        DISP[:, p * BLOCK:(p + 1) * BLOCK] = v
-    outs.append(pltpu.make_async_copy(DISP, do, outsem.at[2]))
-    outs[2].start()
-    for c in outs:
-        c.wait()
+        do[:, p * BLOCK:(p + 1) * BLOCK] = v
 
 
 def per_device(
@@ -402,25 +443,44 @@
         V((3, 2, rows, 128), f32), V((3, 2, rows, 128), f32),
         V((3, 2, L, cols), f32), V((3, 2, L, cols), f32), V((L, cols), f32), V((L, cols), f32),
         V((2, nlon, 1, 128), f32), V((2, nlat, 1, 128), f32),
-        dma((10,)), dma((3,)), dma((3, 5)), dma((3, 5)), dma((2, nlon)), dma((2, nlon)), dma((2, nlat)), dma((2, nlat)),
+        dma((8 + 2 * GROUPS,)), dma((3,)), dma((3, 5)), dma((3, 5)), dma((2, nlon)), dma((2, nlon)), dma((2, nlat)), dma((2, nlat)),
         dma((2,)), dma((2,)),
     ]
     hbm = pl.BlockSpec(memory_space=pl.ANY)
     vmem = pl.BlockSpec(memory_space=pltpu.VMEM)
-    return pl.pallas_call(
+    outs = pl.pallas_call(
         functools.partial(kernel, nlon, nlat),
         out_shape=(
-            jax.ShapeDtypeStruct(full, f32), jax.ShapeDtypeStruct(inter, f32), jax.ShapeDtypeStruct((rows, cols), f32),
+            V(full, f32), V(inter, f32), V((rows, cols), f32),
         ),
         in_specs=[hbm] * 10 + [vmem] * 2,
-        out_specs=(hbm,) * 3,
+        out_specs=(vmem,) * 3,
         scratch_shapes=scratch,
         name="aquifer_step",
-        compiler_params=pltpu.CompilerParams(collective_id=0, has_side_effects=True, vmem_limit_bytes=60 * 1024 * 1024),
+        compiler_params=pltpu.CompilerParams(collective_id=0, has_side_effects=True, vmem_limit_bytes=52 * 1024 * 1024),
     )(
         head, storage, east_cond, north_cond, leakance, recharge, recoverable_skeleton_coefs,
         permanent_skeleton_coefs, critical_heads, cell_flags, kernel_, land_tiles,
     )
+
+    def put(a, b, c, x, y, z, sem):
+        copies = [pltpu.make_async_copy(s, d, sem.at[i]) for i, (s, d) in enumerate(((a, x), (b, y), (c, z)))]
+        for copy in copies:
+            copy.start()
+        for copy in copies:
+            copy.wait()
+
+    return pl.pallas_call(
+        put,
+        out_shape=(
+            jax.ShapeDtypeStruct(full, f32), jax.ShapeDtypeStruct(inter, f32), jax.ShapeDtypeStruct((rows, cols), f32),
+        ),
+        in_specs=[vmem] * 3,
+        out_specs=(hbm,) * 3,
+        scratch_shapes=[dma((3,))],
+        name="put",
+        compiler_params=pltpu.CompilerParams(vmem_limit_bytes=1024 * 1024),
+    )(*outs)
 
 
 def solution(mesh):

time: 49.6 us -> 39.4 us (0.79)
  local copies, waits for them, and re-layouts: 5.45 us -> 0 us
  Pallas kernels: 43.3 us -> 38.5 us
    unnamed x7 -> x0, local copies, waits for them, and re-layouts: 5.45 us -> none
    pallas_call x1 -> x2, Pallas kernels: 43.3 us -> 38.5 us  [the longest x1 36.4 us: per_device(): pl.pallas_call(functools.partial(kernel, nlon, nlat), out_shape=(V(full,...]
where the time goes in v2:
time: 39.4 us; the launch traced here: 39.1 us
  Pallas kernels  38.5 us (98%)
  between operations  0.64 us (2%)
    pallas_call x1, Pallas kernels, per_device(): pl.pallas_call(functools.partial(kernel, nlon, nlat), out_shape=(V(full,...  36.4 us
    pallas_call x1, Pallas kernels, per_device(): pl.pallas_call(put, out_shape=(jax.ShapeDtypeStruct(full, f32), jax.Shape...  2.03 us

profile of v2, /device:TPU:1, one launch (start us, length us, event | category | flops | bytes accessed | tf_op | source)
XLA Modules:
  0.0 39.1 jit_solution(10073988660358945585)
XLA Ops:
  0.6 36.4 %aquifer_step.1 = (f32[4,64,2048]{2,1,0:T(8,128)S(1)}, f32[3,64,2048]{2,1,0:T(8,128)S(1)}, f32[64,2048]{1,0:T(8,128)S(1)}) custom-call(f32[4,64,2048]{2,1,0:T(8,128)} %head.1, f32[4,64,2048]{2,1,0:T(8,128)} %stor.1, f32[4,64,2048]{2,1,0:T(8,128)} %east.1, f32[4,64,2048]{2,1,0:T(8,128)} %north.1, f32[3,64,2048]{2,1,0:T(8,128)} %leak.1, f32[4,64,2048]{2,1,0:T(8,128)} %rech.1, ...), custom_call_target="tpu_custom_call" | custom-call | tf_op jit(solution)/shard_map/aquifer_step/pallas_call | solution.py:451
  37.1 2.0 %put.1 = (f32[4,64,2048]{2,1,0:T(8,128)}, f32[3,64,2048]{2,1,0:T(8,128)}, f32[64,2048]{1,0:T(8,128)}) custom-call(f32[4,64,2048]{2,1,0:T(8,128)S(1)} %get-tuple-element.6.a, f32[3,64,2048]{2,1,0:T(8,128)S(1)} %get-tuple-element.7.b, f32[64,2048]{1,0:T(8,128)S(1)} %get-tuple-element.8.c), custom_call_target="tpu_custom_call" | custom-call | tf_op jit(solution)/shard_map/put/pallas_call | solution.py:473

commit v3 on v2

--- a/solution.py
+++ b/solution.py
@@ -198,10 +198,10 @@
         return centre, out
 
     def fold(v):
-        total = v[:, 0:128]
-        for c in range(128, cols, 128):
-            total = total + v[:, c:c + 128]
-        return total
+        parts = [v[:, c:c + 128] for c in range(0, cols, 128)]
+        while len(parts) > 1:
+            parts = [sum(parts[i:i + 2][1:], parts[i]) for i in range(0, len(parts), 2)]
+        return parts[0]
 
     def all_reduce(t, va, vb):
         a = jnp.sum(va, axis=0, keepdims=True)
@@ -269,9 +269,9 @@
             r = centre[l]
             w = M[l, band(k), :] * (S[l, band(k), :] * r + out[l])
             W[l, band(k), mid] = w
-            a = a + fold(r * r)
-            b = b + fold(r * w)
-        return a, b
+            square = r * r if l == 0 else square + r * r
+            cross = r * w if l == 0 else cross + r * w
+        return a + fold(square), b + fold(cross)
 
     a, b = lax.fori_loop(0, bands, second, (zero, zero))
     b = b + take_halo(1, R, copies, W, 128, 1.0)
@@ -298,9 +298,9 @@
             w = W[l, band(k), mid]
             r1 = R[l, band(k), mid] - alpha_row * w
             s1 = w - alpha_row * Q[l, band(k), :]
-            a = a + fold(r1 * r1)
-            b = b + fold(r1 * s1)
-        return a, b
+            square = r1 * r1 if l == 0 else square + r1 * r1
+            cross = r1 * s1 if l == 0 else cross + r1 * s1
+        return a + fold(square), b + fold(cross)
 
     a, b = lax.fori_loop(0, bands, third, (zero, zero))
     start, middle, finish = all_reduce(1, a, b)

time: 39.4 us -> 39.4 us (level)
  no operation moved by 1% of the time
where the time goes in v3:
time: 39.4 us; the launch traced here: 39.2 us
  Pallas kernels  38.5 us (98%)
  between operations  0.64 us (2%)
    pallas_call x1, Pallas kernels, per_device(): pl.pallas_call(functools.partial(kernel, nlon, nlat), out_shape=(V(full,...  36.5 us
    pallas_call x1, Pallas kernels, per_device(): pl.pallas_call(put, out_shape=(jax.ShapeDtypeStruct(full, f32), jax.Shape...  2.03 us

profile of v3, /device:TPU:1, one launch (start us, length us, event | category | flops | bytes accessed | tf_op | source)
XLA Modules:
  0.0 39.2 jit_solution(552020147080045066)
XLA Ops:
  0.6 36.5 %aquifer_step.1 = (f32[4,64,2048]{2,1,0:T(8,128)S(1)}, f32[3,64,2048]{2,1,0:T(8,128)S(1)}, f32[64,2048]{1,0:T(8,128)S(1)}) custom-call(f32[4,64,2048]{2,1,0:T(8,128)} %head.1, f32[4,64,2048]{2,1,0:T(8,128)} %stor.1, f32[4,64,2048]{2,1,0:T(8,128)} %east.1, f32[4,64,2048]{2,1,0:T(8,128)} %north.1, f32[3,64,2048]{2,1,0:T(8,128)} %leak.1, f32[4,64,2048]{2,1,0:T(8,128)} %rech.1, ...), custom_call_target="tpu_custom_call" | custom-call | tf_op jit(solution)/shard_map/aquifer_step/pallas_call | solution.py:451
  37.1 2.0 %put.1 = (f32[4,64,2048]{2,1,0:T(8,128)}, f32[3,64,2048]{2,1,0:T(8,128)}, f32[64,2048]{1,0:T(8,128)}) custom-call(f32[4,64,2048]{2,1,0:T(8,128)S(1)} %get-tuple-element.6.a, f32[3,64,2048]{2,1,0:T(8,128)S(1)} %get-tuple-element.7.b, f32[64,2048]{1,0:T(8,128)S(1)} %get-tuple-element.8.c), custom_call_target="tpu_custom_call" | custom-call | tf_op jit(solution)/shard_map/put/pallas_call | solution.py:473
